TPU v7x, 32 devices: a whole 2x2x4 slice. The times are simulated.
32 devices in a mesh: patch: 8 (over y, x, core), group: 4 (over z).
Axes of the slice: x: 2, y: 2, z: 4, core: 2. Of those that a mesh axis runs over, the one named last changes fastest.
Arguments:
- grid_latent: bfloat16 [16384, 512], P(('patch', 'group')), may hold values from -6 to 6
- mesh_latent: bfloat16 [8192, 512], P(('patch', 'group')), may hold values from -6 to 6
- cotangent: bfloat16 [8192, 512], P(('patch', 'group')), may hold values from -6 to 6
- halo_rows: int32 [8192], P(('patch', 'group')), may hold values from 0 to 511
- encoder_sender: int32 [24576], P(('patch', 'group')), may hold values from 0 to 767
- encoder_target: int32 [24576], P(('patch', 'group')), may hold values from 0 to 255
- encoder_count: int32 [32], P(('patch', 'group')), may hold values from 96 to 768, as said below
- process_sender: int32 [24576], P(('patch', 'group')), may hold values from 0 to 319
- process_target: int32 [24576], P(('patch', 'group')), may hold values from 0 to 255
- process_count: int32 [32], P(('patch', 'group')), may hold values from 96 to 768, as said below
- encoder_source: bfloat16 [512, 512], replicated, may hold values from -0.25 to 0.25
- encoder_dest: bfloat16 [512, 512], replicated, may hold values from -0.25 to 0.25
- encoder_output: bfloat16 [512, 512], replicated, may hold values from -0.25 to 0.25
- encoder_gain: float32 [512], replicated, may hold values from 0.5 to 1.5
- process_source: bfloat16 [512, 512], replicated, may hold values from -0.25 to 0.25
- process_dest: bfloat16 [512, 512], replicated, may hold values from -0.25 to 0.25
- process_output: bfloat16 [512, 512], replicated, may hold values from -0.25 to 0.25
- process_gain: float32 [512], replicated, may hold values from 0.5 to 1.5
Outputs:
- grid_grad: bfloat16 [16384, 512], P(('patch', 'group'))
- mesh_grad: bfloat16 [8192, 512], P(('patch', 'group'))
Inputs may be any that keep to these rules, and one draw needn't show every extreme that they name: `halo_rows`: a block's entries are rows of its own grid nodes. `encoder_sender`: rows of the block's extended grid table. `encoder_target`: rows of the block's own mesh nodes. The first encoder_count slots of a block are edges, the rest padding; some block is full in every draw. `process_sender`: rows of the block's sender table: its own mesh nodes, then the coarse nodes of its group. `process_target`: rows of the block's own mesh nodes. The first process_count slots of a block are edges, the rest padding; some block is full in every draw.
All inputs are finite; a program needn't handle non-finite values.
Results may differ from a plain program's by a relative error of at most 0.01.
Values may be sent and summed in bfloat16 or wider, within the bound.
No kernel may reach another device: no remote copies, remote signals or barrier semaphores. Data moves between devices by JAX's collectives and lax.ppermute only.
A program may use at most 64 MiB of HBM per device.

v0:
```python
import jax
import jax.numpy as jnp
from jax import lax
from jax.sharding import PartitionSpec as P

EPSILON = 1e-05


def padded_2(x, sides, width):
    for axis, dim in sides:
        size, length = (lax.axis_size(axis), x.shape[dim])
        up = [(i, (i + 1) % size) for i in range(size)]
        down = [(j, i) for i, j in up]
        last = lax.slice_in_dim(x, length - width, length, axis=dim)
        initial = lax.slice_in_dim(x, 0, width, axis=dim)
        before = lax.ppermute(last, axis, up)
        after = lax.ppermute(initial, axis, down)
        x = jnp.concatenate([before, x, after], axis=dim)
    return x


def silu_slope(values):
    logistic = jax.nn.sigmoid(values)
    return logistic * (1.0 + values * (1.0 - logistic))


def norm_forward(values, norm_gain):
    center = values - jnp.mean(values, axis=-1, keepdims=True)
    inverse = lax.rsqrt(jnp.mean(center * center, axis=-1, keepdims=True) + EPSILON)
    normed = center * inverse
    return (normed * norm_gain, normed, inverse)


def norm_backward(grad_out, normed, inverse, norm_gain):
    scaled = grad_out * norm_gain
    return inverse * (
        scaled
        - jnp.mean(scaled, axis=-1, keepdims=True)
        - normed * jnp.mean(scaled * normed, axis=-1, keepdims=True)
    )


def edge_forward(source, dest_proj, sender, target, live_count, out_weight, mesh_count):
    preact = source[sender] + dest_proj[target]
    hidden = jax.nn.silu(preact).astype(jnp.bfloat16)
    message = jnp.dot(hidden, out_weight, preferred_element_type=jnp.float32).astype(jnp.bfloat16)
    live_slots = jnp.arange(sender.shape[0], dtype=jnp.int32) < live_count
    onehot = (
        (target[None, :] == jnp.arange(mesh_count, dtype=jnp.int32)[:, None]) & live_slots[None, :]
    ).astype(jnp.bfloat16)
    gathered = jnp.dot(onehot, message, preferred_element_type=jnp.float32)
    return (gathered, preact, onehot, live_slots)


def edge_backward(
    grad_gathered, preact, onehot, live_slots, sender, target, out_weight, table_rows
):
    grad_message = jnp.where(live_slots[:, None], grad_gathered[target], 0.0).astype(jnp.bfloat16)
    grad_hidden = jnp.dot(grad_message, out_weight.T, preferred_element_type=jnp.float32)
    grad_preact = (grad_hidden * silu_slope(preact)).astype(jnp.bfloat16)
    chooser = (sender[None, :] == jnp.arange(table_rows, dtype=jnp.int32)[:, None]).astype(
        jnp.bfloat16
    )
    grad_source = jnp.dot(chooser, grad_preact, preferred_element_type=jnp.float32)
    grad_dest = jnp.dot(onehot, grad_preact, preferred_element_type=jnp.float32)
    return (grad_source, grad_dest)


def encoder_pass(
    extended,
    mesh_rows,
    sender,
    target,
    live_count,
    source_weight,
    dest_weight,
    out_weight,
    norm_gain,
):
    source = jnp.dot(extended, source_weight, preferred_element_type=jnp.float32)
    dest_proj = jnp.dot(mesh_rows, dest_weight, preferred_element_type=jnp.float32)
    gathered, preact, onehot, live_slots = edge_forward(
        source, dest_proj, sender, target, live_count, out_weight, mesh_rows.shape[0]
    )
    shifted, normed, inverse = norm_forward(gathered, norm_gain)
    updated = (mesh_rows.astype(jnp.float32) + shifted).astype(jnp.bfloat16)
    return (updated, (preact, onehot, live_slots, normed, inverse))


def encoder_backward(
    grad_updated, stored, table_rows, sender, target, dest_weight, out_weight, norm_gain
):
    preact, onehot, live_slots, normed, inverse = stored
    grad_gathered = norm_backward(grad_updated, normed, inverse, norm_gain)
    grad_source, grad_dest = edge_backward(
        grad_gathered, preact, onehot, live_slots, sender, target, out_weight, table_rows
    )
    mesh_grad = grad_updated + jnp.dot(
        grad_dest.astype(jnp.bfloat16), dest_weight.T, preferred_element_type=jnp.float32
    )
    return (mesh_grad, grad_source.astype(jnp.bfloat16))


def process_grads(
    updated,
    coarse_proj,
    sender,
    target,
    live_count,
    cotangent,
    source_weight,
    dest_weight,
    out_weight,
    norm_gain,
):
    local_proj = jnp.dot(updated, source_weight, preferred_element_type=jnp.float32)
    source = jnp.concatenate([local_proj, coarse_proj], axis=0)
    dest_proj = jnp.dot(updated, dest_weight, preferred_element_type=jnp.float32)
    gathered, preact, onehot, live_slots = edge_forward(
        source, dest_proj, sender, target, live_count, out_weight, updated.shape[0]
    )
    unused, normed, inverse = norm_forward(gathered, norm_gain)
    grad_out = cotangent.astype(jnp.float32)
    grad_gathered = norm_backward(grad_out, normed, inverse, norm_gain)
    grad_source, grad_dest = edge_backward(
        grad_gathered, preact, onehot, live_slots, sender, target, out_weight, source.shape[0]
    )
    mesh_count = updated.shape[0]
    grad_local = grad_out + jnp.dot(
        grad_source[:mesh_count].astype(jnp.bfloat16),
        source_weight.T,
        preferred_element_type=jnp.float32,
    )
    grad_local = grad_local + jnp.dot(
        grad_dest.astype(jnp.bfloat16), dest_weight.T, preferred_element_type=jnp.float32
    )
    return (grad_local, grad_source[mesh_count:])


def on_device(
    grid_latent,
    mesh_latent,
    cotangent,
    halo_rows,
    encoder_sender,
    encoder_target,
    encoder_count,
    process_sender,
    process_target,
    process_count,
    encoder_source,
    encoder_dest,
    encoder_output,
    encoder_gain,
    process_source,
    process_dest,
    process_output,
    process_gain,
):
    rim_size = halo_rows.shape[0] // 2
    grid_rows = grid_latent.shape[0]
    outgoing = grid_latent[halo_rows]
    padded = padded_2(outgoing, (("patch", 0),), rim_size)
    extended = jnp.concatenate([grid_latent, padded[:rim_size], padded[3 * rim_size :]], axis=0)
    updated, stored = encoder_pass(
        extended,
        mesh_latent,
        encoder_sender,
        encoder_target,
        encoder_count[0],
        encoder_source,
        encoder_dest,
        encoder_output,
        encoder_gain,
    )
    coarse_rows = mesh_latent.shape[0] // 16
    coarse_proj = jnp.dot(
        lax.all_gather(updated[:coarse_rows], "group", axis=0, tiled=True),
        process_source,
        preferred_element_type=jnp.float32,
    )
    grad_local, grad_coarse = process_grads(
        updated,
        coarse_proj,
        process_sender,
        process_target,
        process_count[0],
        cotangent,
        process_source,
        process_dest,
        process_output,
        process_gain,
    )
    back_weight = process_source.astype(jnp.float32).T
    coarse_grad = lax.psum_scatter(
        jnp.dot(
            grad_coarse,
            back_weight,
            precision=lax.Precision.HIGHEST,
            preferred_element_type=jnp.float32,
        ),
        "group",
        scatter_dimension=0,
        tiled=True,
    )
    grad_updated = grad_local.at[:coarse_rows].add(coarse_grad)
    mesh_grad, source_grads = encoder_backward(
        grad_updated,
        stored,
        extended.shape[0],
        encoder_sender,
        encoder_target,
        encoder_dest,
        encoder_output,
        encoder_gain,
    )
    own_grad = jnp.dot(
        source_grads[:grid_rows], encoder_source.T, preferred_element_type=jnp.float32
    )
    returned = padded_2(source_grads[grid_rows:], (("patch", 0),), rim_size)
    peer_sources = jnp.concatenate([returned[:rim_size], returned[3 * rim_size :]], axis=0)
    from_peers = jnp.dot(peer_sources, encoder_source.T, preferred_element_type=jnp.float32)
    grid_grad = own_grad.at[halo_rows].add(from_peers)
    return (grid_grad.astype(jnp.bfloat16), mesh_grad.astype(jnp.bfloat16))


def solution(mesh):
    return jax.shard_map(
        on_device,
        mesh=mesh,
        in_specs=(
            P(("patch", "group"), None),
            P(("patch", "group"), None),
            P(("patch", "group"), None),
            P(("patch", "group")),
            P(("patch", "group")),
            P(("patch", "group")),
            P(("patch", "group")),
            P(("patch", "group")),
            P(("patch", "group")),
            P(("patch", "group")),
            P(),
            P(),
            P(),
            P(),
            P(),
            P(),
            P(),
            P(),
        ),
        out_specs=(P(("patch", "group"), None), P(("patch", "group"), None)),
        check_vma=False,
    )
```

profile of v0, /device:TPU:1, one launch (start us, length us, event | category | flops | bytes accessed | tf_op | source)
XLA Modules:
  0.0 108.4 jit_solution(11747875148235382991)
XLA Ops:
  7.3 0.8 compare_select_fusion.4
  8.1 0.6 copy-done.13
  8.7 2.3 %gather_fusion = bf16[256,512]{1,0:T(8,128)(2,1)S(1)} fusion(bf16[512,512]{1,0:T(8,128)(2,1)} %param.20, s32[1024]{0:T(1024)S(1)} %pad_clamp_fusion.4), kind=kCustom, calls=%fused_computation | custom fusion | bytes 525312 | tf_op jit(solution)/shard_map/gather | solution.py:162
  11.0 2.6 %collective-permute-start = (bf16[128,512]{1,0:T(8,128)(2,1)S(1)}, bf16[128,512]{1,0:T(8,128)(2,1)S(1)}, u32[]{:S(2)}, u32[]{:S(2)}) collective-permute-start(bf16[128,512]{1,0:T(8,128)(2,1)S(1)} %get-tuple-element.20), channel_id=1, source_target_pairs={{0,4},{4,8},{8,12},{12,16},{16,20},{20,24},{24,28},{28,0},{1,5},{5... | collective-permute-start | bytes 393224 | tf_op jit(solution)/shard_map/ppermute | solution.py:16
  15.5 3.1 %gather_fusion.2 = f32[768,512]{1,0:T(8,128)} fusion(f32[256,512]{1,0:T(8,128)S(1)} %fusion.69, s32[1024]{0:T(1024)S(1)} %pad_clamp_fusion.2), kind=kCustom, calls=%fused_computation.2 | custom fusion | bytes 3148800 | tf_op jit(solution)/shard_map/gather | solution.py:44
  18.6 0.6 fusion.7
  19.2 3.1 %gather_fusion.1 = f32[768,512]{1,0:T(8,128)} fusion(f32[768,512]{1,0:T(8,128)S(1)} %fusion.7, s32[1024]{0:T(1024)S(1)} %pad_clamp_fusion.3), kind=kCustom, calls=%fused_computation.1 | custom fusion | bytes 3148800 | tf_op jit(solution)/shard_map/gather | solution.py:44
  22.3 2.9 %fusion.67 = (f32[256]{0:T(256)S(1)}, f32[256,512]{1,0:T(8,128)S(1)}) fusion(bf16[512,512]{1,0:T(8,128)(2,1)} %param.32, f32[768,512]{1,0:T(8,128)} %gather_fusion.1, f32[768,512]{1,0:T(8,128)} %gather_fusion.2, s32[768]{0:T(1024)S(1)} %copy-done.18, pred[768]{0:T(1024)(128)(4,1)S(1)} %iota_compare_fusion.9), kind=kOutput, calls=%fused_computation.111 | convolution fusion | flops 607256320 | bytes 4199168 | tf_op jit(solution)/shard_map/dot_general | solution.py:51
  25.7 10.7 %all_gather.3 = bf16[64,512]{1,0:T(8,128)(2,1)S(1)} all-gather(bf16[16,512]{1,0:T(8,128)(2,1)S(1)} %slice.72), channel_id=1, replica_groups=mesh['patch'=8,'group'=4] {'group'}, dimensions={0}, use_global_device_ids=true | all-gather | bytes 81920 | tf_op jit(solution)/shard_map/all_gather | solution.py:178
  37.3 3.1 %gather_fusion.3 = f32[768,512]{1,0:T(8,128)} fusion(f32[320,512]{1,0:T(8,128)S(1)} %pad_maximum_fusion, s32[1024]{0:T(1024)S(1)} %pad_clamp_fusion.1), kind=kCustom, calls=%fused_computation.3 | custom fusion | bytes 3148800 | tf_op jit(solution)/shard_map/gather | solution.py:44
  40.4 3.1 %gather_fusion.4 = f32[768,512]{1,0:T(8,128)} fusion(f32[256,512]{1,0:T(8,128)S(1)} %fusion.72, s32[1024]{0:T(1024)S(1)} %pad_clamp_fusion), kind=kCustom, calls=%fused_computation.4 | custom fusion | bytes 3148800 | tf_op jit(solution)/shard_map/gather | solution.py:44
  43.5 2.9 %fusion.68 = (f32[256]{0:T(256)S(1)}, f32[256,512]{1,0:T(8,128)S(1)}) fusion(bf16[512,512]{1,0:T(8,128)(2,1)} %param.36, f32[768,512]{1,0:T(8,128)} %gather_fusion.3, f32[768,512]{1,0:T(8,128)} %gather_fusion.4, s32[768]{0:T(1024)S(1)} %copy-done.10, pred[768]{0:T(1024)(128)(4,1)S(1)} %iota_compare_fusion.8), kind=kOutput, calls=%fused_computation.112 | convolution fusion | flops 607256320 | bytes 4199168 | tf_op jit(solution)/shard_map/dot_general | solution.py:51
  47.1 3.3 %gather_fusion.5 = bf16[768,512]{1,0:T(8,128)(2,1)} fusion(bf16[256,512]{1,0:T(8,128)(2,1)S(1)} %fusion.33, s32[1024]{0:T(1024)S(1)} %pad_clamp_fusion), kind=kCustom, calls=%fused_computation.5 | custom fusion | bytes 1575936 | tf_op jit(solution)/shard_map/gather | solution.py:58
  50.5 3.2 %multiply_convert_fusion.1 = bf16[768,512]{1,0:T(8,128)(2,1)S(1)} fusion(bf16[512,512]{1,0:T(8,128)(2,1)} %param.36, bf16[768,512]{1,0:T(8,128)(2,1)} %gather_fusion.5, pred[768]{0:T(1024)(128)(4,1)S(1)} %iota_compare_fusion.8, f32[768,512]{1,0:T(8,128)} %gather_fusion.3, f32[768,512]{1,0:T(8,128)} %gather_fusion.4), kind=kOutput, calls=%fused_computation.12 | convolution fusion | flops 406978560 | bytes 5243648 | tf_op jit(solution)/shard_map/dot_general | solution.py:59
  53.7 0.9 copy-done.6
  54.6 0.4 fusion.6
  55.0 1.3 %fusion.54 = f32[64,512]{1,0:T(8,128)} fusion(bf16[512,512]{1,0:T(8,128)(2,1)S(1)} %copy-done.1, f32[320,512]{1,0:T(8,128)S(1)} %fusion.6), kind=kOutput, calls=%fused_computation.79 | convolution fusion | flops 201326592 | bytes 786432 | tf_op jit(solution)/shard_map/dot_general | solution.py:196
  56.3 0.3 convolution_add_fusion.2
  56.6 1.7 %convolution_add_fusion.1 = f32[256,512]{1,0:T(8,128)S(1)} fusion(f32[256,512]{1,0:T(8,128)S(1)} %convolution_add_fusion.2, bf16[512,512]{1,0:T(8,128)(2,1)S(1)} %copy-done.4, bf16[768,512]{1,0:T(8,128)(2,1)} %copy-done.6, s32[768]{0:T(1024)S(1)} %copy-done.10, pred[768]{0:T(1024)(128)(4,1)} %copy-done.22), kind=kOutput, calls=%fused_computation.24 | convolution fusion | flops 336199680 | bytes 2363136 | tf_op jit(solution)/shard_map/dot_general | solution.py:134
  58.4 19.3 %reduce-scatter.2.cloned.1.call-done = f32[16,512]{1,0:T(8,128)} async-done(((f32[64,512]{1,0:T(8,128)}), f32[16,512]{1,0:T(8,128)}) %reduce-scatter.2.cloned.1.call-update) | async-done | bytes 32784 | tf_op jit(solution)/shard_map/reduce_scatter | solution.py:195
  77.7 0.8 fusion.56
  79.0 2.7 %gather_fusion.6 = bf16[768,512]{1,0:T(8,128)(2,1)S(1)} fusion(bf16[256,512]{1,0:T(8,128)(2,1)S(1)} %subtract_multiply_fusion, s32[1024]{0:T(1024)S(1)} %pad_clamp_fusion.2), kind=kCustom, calls=%fused_computation.6 | custom fusion | bytes 1575936 | tf_op jit(solution)/shard_map/gather | solution.py:58
  81.7 3.7 %multiply_convert_fusion = bf16[768,512]{1,0:T(8,128)(2,1)} fusion(bf16[512,512]{1,0:T(8,128)(2,1)S(1)} %copy-done.23, bf16[768,512]{1,0:T(8,128)(2,1)S(1)} %gather_fusion.6, pred[768]{0:T(1024)(128)(4,1)S(1)} %copy-done.25, f32[768,512]{1,0:T(8,128)} %gather_fusion.1, f32[768,512]{1,0:T(8,128)} %gather_fusion.2), kind=kOutput, calls=%fused_computation.10 | convolution fusion | flops 406978560 | bytes 5243648 | tf_op jit(solution)/shard_map/dot_general | solution.py:59
  85.5 2.5 %fusion.4 = bf16[256,512]{1,0:T(8,128)(2,1)} fusion(f32[256,512]{1,0:T(8,128)S(1)} %fusion.56, bf16[512,512]{1,0:T(8,128)(2,1)S(1)} %copy-done.8, bf16[768,512]{1,0:T(8,128)(2,1)} %multiply_convert_fusion, s32[768]{0:T(1024)S(1)} %copy-done.19, pred[768]{0:T(1024)(128)(4,1)S(1)} %copy-done.25), kind=kOutput, calls=%fused_computation.26 | convolution fusion | flops 336330752 | bytes 2100992 | tf_op jit(solution)/shard_map/dot_general | solution.py:98
  88.0 0.8 fusion.1
  88.8 4.1 %collective-permute-start.2 = (bf16[128,512]{1,0:T(8,128)(2,1)S(1)}, bf16[128,512]{1,0:T(8,128)(2,1)S(1)}, u32[]{:S(2)}, u32[]{:S(2)}) collective-permute-start(bf16[128,512]{1,0:T(8,128)(2,1)S(1)} %get-tuple-element.18), channel_id=1, source_target_pairs={{0,4},{4,8},{8,12},{12,16},{16,20},{20,24},{24,28},{28,0},{1,5},{5... | collective-permute-start | bytes 393224 | tf_op jit(solution)/shard_map/ppermute | solution.py:16
  92.9 0.5 fusion.35
  93.4 1.5 %collective-permute-done.2 = bf16[128,512]{1,0:T(8,128)(2,1)S(1)} collective-permute-done((bf16[128,512]{1,0:T(8,128)(2,1)S(1)}, bf16[128,512]{1,0:T(8,128)(2,1)S(1)}, u32[]{:S(2)}, u32[]{:S(2)}) %collective-permute-start.2) | collective-permute-done | bytes 131104 | tf_op jit(solution)/shard_map/ppermute | solution.py:16
  94.9 3.0 %collective-permute-done.3 = bf16[128,512]{1,0:T(8,128)(2,1)S(1)} collective-permute-done((bf16[128,512]{1,0:T(8,128)(2,1)S(1)}, bf16[128,512]{1,0:T(8,128)(2,1)S(1)}, u32[]{:S(2)}, u32[]{:S(2)}) %collective-permute-start.3) | collective-permute-done | bytes 131104 | tf_op jit(solution)/shard_map/ppermute | solution.py:17
  97.9 0.3 fusion.50
  98.2 2.5 %scatter_fusion = f32[512,512]{1,0:T(8,128)S(1)} fusion(f32[512,512]{1,0:T(8,128)S(1)} %fusion.35, s32[256]{0:T(256)S(1)} %copy-done.14, f32[256,512]{1,0:T(8,128)S(1)} %fusion.50), kind=kCustom, calls=%fused_computation.7 | custom fusion | flops 131072 | bytes 1573888 | tf_op jit(solution)/shard_map/scatter-add | solution.py:223
  100.7 0.9 convert_element_type.67
  (91 shorter events, 3.0 us)
Async XLA Ops:
  7.2 11.5 %copy-start = (bf16[512,512]{1,0:T(8,128)(2,1)S(1)}, bf16[512,512]{1,0:T(8,128)(2,1)}, u32[]{:S(2)}) copy-start(bf16[512,512]{1,0:T(8,128)(2,1)} %param.30) | copy-start | bytes 1572868
  7.2 7.8 %copy-start.20 = (s32[768]{0:T(1024)S(1)}, s32[768]{0:T(1024)}, u32[]{:S(2)}) copy-start(s32[768]{0:T(1024)} %param.24) | copy-start | bytes 9220
  7.2 7.8 %copy-start.16 = (s32[768]{0:T(1024)S(1)}, s32[768]{0:T(1024)}, u32[]{:S(2)}) copy-start(s32[768]{0:T(1024)} %param.27) | copy-start | bytes 9220
  7.2 7.9 %copy-start.18 = (s32[768]{0:T(1024)S(1)}, s32[768]{0:T(1024)}, u32[]{:S(2)}) copy-start(s32[768]{0:T(1024)} %param.25) | copy-start | bytes 9220
  7.2 7.9 %copy-start.10 = (s32[768]{0:T(1024)S(1)}, s32[768]{0:T(1024)}, u32[]{:S(2)}) copy-start(s32[768]{0:T(1024)} %param.28) | copy-start | bytes 9220
  7.2 7.9 %copy-start.7 = (bf16[512,512]{1,0:T(8,128)(2,1)S(1)}, bf16[512,512]{1,0:T(8,128)(2,1)}, u32[]{:S(2)}) copy-start(bf16[512,512]{1,0:T(8,128)(2,1)} %param.31) | copy-start | bytes 1572868
  7.2 7.9 %copy-start.5 = (bf16[256,512]{1,0:T(8,128)(2,1)S(1)}, bf16[256,512]{1,0:T(8,128)(2,1)}, u32[]{:S(2)}) copy-start(bf16[256,512]{1,0:T(8,128)(2,1)} %param.21) | copy-start | bytes 786436
  7.2 70.4 %reduce-scatter.2.cloned.1.call-start = ((), (), s32[]{:S(2)}) async-start(), calls=%async_computation.1 | async-start | bytes 163840 | tf_op jit(solution)/shard_map/reduce_scatter | solution.py:195
  8.1 0.6 copy-start.13
  11.0 7.6 %collective-permute-start = (bf16[128,512]{1,0:T(8,128)(2,1)S(1)}, bf16[128,512]{1,0:T(8,128)(2,1)S(1)}, u32[]{:S(2)}, u32[]{:S(2)}) collective-permute-start(bf16[128,512]{1,0:T(8,128)(2,1)S(1)} %get-tuple-element.20), channel_id=1, source_target_pairs={{0,4},{4,8},{8,12},{12,16},{16,20},{20,24},{24,28},{28,0},{1,5},{5... | collective-permute-start | bytes 393224 | tf_op jit(solution)/shard_map/ppermute | solution.py:16
  13.7 5.0 %collective-permute-start.1 = (bf16[128,512]{1,0:T(8,128)(2,1)S(1)}, bf16[128,512]{1,0:T(8,128)(2,1)S(1)}, u32[]{:S(2)}, u32[]{:S(2)}) collective-permute-start(bf16[128,512]{1,0:T(8,128)(2,1)S(1)} %get-tuple-element.21), channel_id=1, source_target_pairs={{4,0},{8,4},{12,8},{16,12},{20,16},{24,20},{28,24},{0,28},{5,1},{9... | collective-permute-start | bytes 393224 | tf_op jit(solution)/shard_map/ppermute | solution.py:17
  15.0 7.3 %copy-start.24 = (pred[768]{0:T(1024)(128)(4,1)}, pred[768]{0:T(1024)(128)(4,1)S(1)}, u32[]{:S(2)}) copy-start(pred[768]{0:T(1024)(128)(4,1)S(1)} %iota_compare_fusion.9) | copy-start | bytes 2308
  15.4 35.0 %copy-start.22 = (pred[768]{0:T(1024)(128)(4,1)}, pred[768]{0:T(1024)(128)(4,1)S(1)}, u32[]{:S(2)}) copy-start(pred[768]{0:T(1024)(128)(4,1)S(1)} %iota_compare_fusion.8) | copy-start | bytes 2308
  15.5 3.2 %copy-start.2 = (bf16[512,512]{1,0:T(8,128)(2,1)S(1)}, bf16[512,512]{1,0:T(8,128)(2,1)}, u32[]{:S(2)}) copy-start(bf16[512,512]{1,0:T(8,128)(2,1)} %param.20) | copy-start | bytes 1572868
  22.3 3.1 %copy-start.9 = (f32[512]{0:T(512)S(1)}, f32[512]{0:T(512)}, u32[]{:S(2)}) copy-start(f32[512]{0:T(512)} %param.33) | copy-start | bytes 6148
  25.2 11.2 %copy-start.1 = (bf16[512,512]{1,0:T(8,128)(2,1)S(1)}, bf16[512,512]{1,0:T(8,128)(2,1)}, u32[]{:S(2)}) copy-start(bf16[512,512]{1,0:T(8,128)(2,1)} %param.34) | copy-start | bytes 1572868
  25.4 11.5 %copy-start.11 = (f32[256]{0:T(256)}, f32[256]{0:T(256)S(1)}, u32[]{:S(2)}) copy-start(f32[256]{0:T(256)S(1)} %add_rsqrt_fusion.1) | copy-start | bytes 3076
  25.5 11.5 %copy-start.4 = (bf16[512,512]{1,0:T(8,128)(2,1)S(1)}, bf16[512,512]{1,0:T(8,128)(2,1)}, u32[]{:S(2)}) copy-start(bf16[512,512]{1,0:T(8,128)(2,1)} %param.35) | copy-start | bytes 1572868
  43.5 3.2 %copy-start.3 = (bf16[256,512]{1,0:T(8,128)(2,1)S(1)}, bf16[256,512]{1,0:T(8,128)(2,1)}, u32[]{:S(2)}) copy-start(bf16[256,512]{1,0:T(8,128)(2,1)} %param.22) | copy-start | bytes 786436
  43.5 3.2 %copy-start.15 = (f32[512]{0:T(512)S(1)}, f32[512]{0:T(512)}, u32[]{:S(2)}) copy-start(f32[512]{0:T(512)} %param.37) | copy-start | bytes 6148
  50.5 4.1 %copy-start.17 = (s32[768]{0:T(1024)S(1)}, s32[768]{0:T(1024)}, u32[]{:S(2)}) copy-start(s32[768]{0:T(1024)} %param.27) | copy-start | bytes 9220
  53.7 0.9 copy-start.6
  56.6 21.9 %copy-start.12 = (f32[256]{0:T(256)S(1)}, f32[256]{0:T(256)}, u32[]{:S(2)}) copy-start(f32[256]{0:T(256)} %copy-done.11) | copy-start | bytes 3076
  78.9 2.7 %copy-start.23 = (bf16[512,512]{1,0:T(8,128)(2,1)S(1)}, bf16[512,512]{1,0:T(8,128)(2,1)}, u32[]{:S(2)}) copy-start(bf16[512,512]{1,0:T(8,128)(2,1)} %param.32) | copy-start | bytes 1572868
  79.0 2.7 %copy-start.25 = (pred[768]{0:T(1024)(128)(4,1)S(1)}, pred[768]{0:T(1024)(128)(4,1)}, u32[]{:S(2)}) copy-start(pred[768]{0:T(1024)(128)(4,1)} %copy-done.24) | copy-start | bytes 2308
  81.7 3.8 %copy-start.8 = (bf16[512,512]{1,0:T(8,128)(2,1)S(1)}, bf16[512,512]{1,0:T(8,128)(2,1)}, u32[]{:S(2)}) copy-start(bf16[512,512]{1,0:T(8,128)(2,1)} %param.31) | copy-start | bytes 1572868
  81.7 3.8 %copy-start.19 = (s32[768]{0:T(1024)S(1)}, s32[768]{0:T(1024)}, u32[]{:S(2)}) copy-start(s32[768]{0:T(1024)} %param.25) | copy-start | bytes 9220
  85.5 2.5 %copy-start.21 = (s32[768]{0:T(1024)S(1)}, s32[768]{0:T(1024)}, u32[]{:S(2)}) copy-start(s32[768]{0:T(1024)} %param.24) | copy-start | bytes 9220
  85.5 2.5 %copy-start.26 = (bf16[768,512]{1,0:T(8,128)(2,1)S(1)}, bf16[768,512]{1,0:T(8,128)(2,1)}, u32[]{:S(2)}) copy-start(bf16[768,512]{1,0:T(8,128)(2,1)} %multiply_convert_fusion) | copy-start | bytes 2359300
  88.8 6.1 %collective-permute-start.2 = (bf16[128,512]{1,0:T(8,128)(2,1)S(1)}, bf16[128,512]{1,0:T(8,128)(2,1)S(1)}, u32[]{:S(2)}, u32[]{:S(2)}) collective-permute-start(bf16[128,512]{1,0:T(8,128)(2,1)S(1)} %get-tuple-element.18), channel_id=1, source_target_pairs={{0,4},{4,8},{8,12},{12,16},{16,20},{20,24},{24,28},{28,0},{1,5},{5... | collective-permute-start | bytes 393224 | tf_op jit(solution)/shard_map/ppermute | solution.py:16
  92.9 5.3 %copy-start.14 = (s32[256]{0:T(256)S(1)}, s32[256]{0:T(256)}, u32[]{:S(2)}) copy-start(s32[256]{0:T(256)} %copy-done.13) | copy-start | bytes 3076
  92.9 4.9 %collective-permute-start.3 = (bf16[128,512]{1,0:T(8,128)(2,1)S(1)}, bf16[128,512]{1,0:T(8,128)(2,1)S(1)}, u32[]{:S(2)}, u32[]{:S(2)}) collective-permute-start(bf16[128,512]{1,0:T(8,128)(2,1)S(1)} %get-tuple-element.19), channel_id=1, source_target_pairs={{4,0},{8,4},{12,8},{16,12},{20,16},{24,20},{28,24},{0,28},{5,1},{9... | collective-permute-start | bytes 393224 | tf_op jit(solution)/shard_map/ppermute | solution.py:17
Sparse Core Ops, SparseCore 0:
  56.8 20.8 reduce-scatter.1
where the time goes:
time: 109 us; the launch traced here: 108 us
  waiting for transfers between devices  23.8 us (22%)
  local copies, waits for them, and re-layouts  22.4 us (21%)
  matrix products  22.2 us (20%)
  between operations  15.9 us (15%)
  blocking collectives  10.7 us (10%)
  starting transfers between devices  6.83 us (6%)
  other arithmetic  6.52 us (6%)
    reduce_scatter x1, waiting for transfers between devices, on_device(): lax.psum_scatter(jnp.dot(grad_coarse, back_weight, precision=lax.Precisio...  19.3 us
    gather x4, local copies, waits for them, and re-layouts, edge_forward(): preact = source[sender] + dest_proj[target]  12.5 us
    all_gather x1, blocking collectives, on_device(): lax.all_gather(updated[:coarse_rows], 'group', axis=0, tiled=True)  10.7 us
    dot_general x2, matrix products, edge_backward(): jnp.dot(grad_message, out_weight.T, preferred_element_type=jnp.float32)  6.96 us
    ppermute x2, starting transfers between devices, padded_2(): before = lax.ppermute(last, axis, up)  6.78 us
    gather x2, local copies, waits for them, and re-layouts, edge_backward(): grad_gathered[target]  6 us
    dot_general x2, matrix products, edge_forward(): gathered = jnp.dot(onehot, message, preferred_element_type=jnp.float32)  5.79 us
    ppermute x2, waiting for transfers between devices, padded_2(): after = lax.ppermute(initial, axis, down)  3.03 us
  transfers between devices with their start and end apart: 5, of which 3 were waited for; matrix products, arithmetic and copies ran while one was open for 5% of the time, Pallas kernels for 0%

commit v1 on v0

--- a/solution.py
+++ b/solution.py
@@ -4,6 +4,12 @@
 from jax.sharding import PartitionSpec as P
 
 EPSILON = 1e-05
+
+
+def _push_scenes(load, in_dim):
+    load = jnp.moveaxis(load, 0, in_dim)
+    ready = load.shape
+    return load.reshape(*ready[:in_dim], ready[in_dim] * ready[in_dim + 1], *ready[in_dim + 2 :])
 
 
 def padded_2(x, sides, width):
@@ -174,8 +180,30 @@
         encoder_gain,
     )
     coarse_rows = mesh_latent.shape[0] // 16
+
+    def pair_spans(view, ax_name, join_dim):
+        axis_len = lax.axis_size(ax_name)
+        store = [(ii, (ii + 1) % axis_len) for ii in range(axis_len)]
+        found = [(jj, idx) for idx, jj in store]
+        block_last, y_new = ([], [])
+        d = 0
+        while d < axis_len - 1:
+            if d % 2 == 0:
+                a_now = lax.ppermute(block_last[-1] if block_last else view, ax_name, store)
+                block_last.append(a_now)
+            else:
+                f_next = lax.ppermute(y_new[-1] if y_new else view, ax_name, found)
+                y_new.append(f_next)
+            d = d + 1
+        state_next = jnp.stack([*block_last[::-1], view, *y_new], axis=0)
+        opened = lax.axis_index(ax_name)
+        all_rows = len(block_last)
+        z2 = opened - all_rows
+        state_next = state_next[(jnp.arange(axis_len) - z2) % axis_len]
+        return _push_scenes(state_next, join_dim)
+
     coarse_proj = jnp.dot(
-        lax.all_gather(updated[:coarse_rows], "group", axis=0, tiled=True),
+        pair_spans(updated[:coarse_rows], "group", 0),
         process_source,
         preferred_element_type=jnp.float32,
     )

time: 109 us -> 105 us (0.963)
  blocking collectives: 10.7 us -> 0 us
  starting transfers between devices: 6.83 us -> 10.2 us
  waiting for transfers between devices: 23.8 us -> 27 us
    all_gather x1 -> x0, blocking collectives: 10.7 us -> none  [on_device(): lax.all_gather(updated[:coarse_rows], 'group', axis=0, tiled=True)]
    ppermute x0 -> x3, waiting for transfers between devices: none -> 5.02 us  [the longest x2 5.02 us: pair_spans(): a_now = lax.ppermute(block_last[-1] if block_last else view, ax_name, store)]
    ppermute x0 -> x3, starting transfers between devices: none -> 3.37 us  [the longest x1 3.36 us: pair_spans(): f_next = lax.ppermute(y_new[-1] if y_new else view, ax_name, found)]
    reduce_scatter x1, waiting for transfers between devices: 19.3 us -> 17.4 us  [on_device(): lax.psum_scatter(jnp.dot(grad_coarse, back_weight, precision=lax.Precisio...]
  transfers between devices with their start and end apart: 5 -> 8, of which waited for: 3 -> 5; matrix products, arithmetic and copies ran while one was open for 5% -> 9% of each run, Pallas kernels for 0% -> 0%
where the time goes in v1:
time: 105 us
  waiting for transfers between devices  27 us (26%)
  local copies, waits for them, and re-layouts  23 us (22%)
  matrix products  22.3 us (21%)
  between operations  15.9 us (15%)
  starting transfers between devices  10.2 us (10%)
  other arithmetic  6.55 us (6%)
    reduce_scatter x1, waiting for transfers between devices, on_device(): lax.psum_scatter(jnp.dot(grad_coarse, back_weight, precision=lax.Precisio...  17.4 us
    gather x4, local copies, waits for them, and re-layouts, edge_forward(): preact = source[sender] + dest_proj[target]  12.5 us
    dot_general x2, matrix products, edge_backward(): jnp.dot(grad_message, out_weight.T, preferred_element_type=jnp.float32)  6.96 us
    ppermute x2, starting transfers between devices, padded_2(): before = lax.ppermute(last, axis, up)  6.84 us
    gather x2, local copies, waits for them, and re-layouts, edge_backward(): grad_gathered[target]  6.02 us
    dot_general x2, matrix products, edge_forward(): gathered = jnp.dot(onehot, message, preferred_element_type=jnp.float32)  5.8 us
    ppermute x2, waiting for transfers between devices, pair_spans(): a_now = lax.ppermute(block_last[-1] if block_last else view, ax_name, store)  5.02 us
    ppermute x1, starting transfers between devices, pair_spans(): f_next = lax.ppermute(y_new[-1] if y_new else view, ax_name, found)  3.36 us
  transfers between devices with their start and end apart: 8, of which 5 were waited for; matrix products, arithmetic and copies ran while one was open for 9% of the time, Pallas kernels for 0%

profile of v1, /device:TPU:1, one launch (start us, length us, event | category | flops | bytes accessed | tf_op | source)
XLA Modules:
  0.0 105.0 jit_solution(16233820574141950155)
XLA Ops:
  7.3 0.8 compare_select_fusion.4
  8.1 0.6 copy-done.13
  8.7 2.3 %gather_fusion = bf16[256,512]{1,0:T(8,128)(2,1)S(1)} fusion(bf16[512,512]{1,0:T(8,128)(2,1)} %param.20, s32[1024]{0:T(1024)S(1)} %pad_clamp_fusion.5), kind=kCustom, calls=%fused_computation | custom fusion | bytes 525312 | tf_op jit(solution)/shard_map/gather | solution.py:168
  11.0 2.6 %collective-permute-start = (bf16[128,512]{1,0:T(8,128)(2,1)S(1)}, bf16[128,512]{1,0:T(8,128)(2,1)S(1)}, u32[]{:S(2)}, u32[]{:S(2)}) collective-permute-start(bf16[128,512]{1,0:T(8,128)(2,1)S(1)} %get-tuple-element.22), channel_id=1, source_target_pairs={{0,4},{4,8},{8,12},{12,16},{16,20},{20,24},{24,28},{28,0},{1,5},{5... | collective-permute-start | bytes 393224 | tf_op jit(solution)/shard_map/ppermute | solution.py:22
  15.5 3.1 %gather_fusion.2 = f32[768,512]{1,0:T(8,128)} fusion(f32[256,512]{1,0:T(8,128)S(1)} %fusion.71, s32[1024]{0:T(1024)S(1)} %pad_clamp_fusion.3), kind=kCustom, calls=%fused_computation.2 | custom fusion | bytes 3148800 | tf_op jit(solution)/shard_map/gather | solution.py:50
  18.7 0.6 fusion.7
  19.3 3.1 %gather_fusion.1 = f32[768,512]{1,0:T(8,128)} fusion(f32[768,512]{1,0:T(8,128)S(1)} %fusion.7, s32[1024]{0:T(1024)S(1)} %pad_clamp_fusion.4), kind=kCustom, calls=%fused_computation.1 | custom fusion | bytes 3148800 | tf_op jit(solution)/shard_map/gather | solution.py:50
  22.4 2.9 %fusion.69 = (f32[256]{0:T(256)S(1)}, f32[256,512]{1,0:T(8,128)S(1)}) fusion(bf16[512,512]{1,0:T(8,128)(2,1)} %param.32, f32[768,512]{1,0:T(8,128)} %gather_fusion.1, f32[768,512]{1,0:T(8,128)} %gather_fusion.2, s32[768]{0:T(1024)S(1)} %copy-done.18, pred[768]{0:T(1024)(128)(4,1)S(1)} %iota_compare_fusion.9), kind=kOutput, calls=%fused_computation.121 | convolution fusion | flops 607256320 | bytes 4199168 | tf_op jit(solution)/shard_map/dot_general | solution.py:57
  25.7 3.4 %collective-permute-start.4 = (bf16[16,512]{1,0:T(8,128)(2,1)S(1)}, bf16[16,512]{1,0:T(8,128)(2,1)S(1)}, u32[]{:S(2)}, u32[]{:S(2)}) collective-permute-start(bf16[16,512]{1,0:T(8,128)(2,1)S(1)} %get-tuple-element.21), channel_id=1, source_target_pairs={{1,0},{2,1},{3,2},{0,3},{5,4},{6,5},{7,6},{4,7},{9,8},{10,9},{11,1... | collective-permute-start | bytes 49160 | tf_op jit(solution)/shard_map/ppermute | solution.py:195
  29.4 4.1 %collective-permute-done.2 = bf16[16,512]{1,0:T(8,128)(2,1)S(1)} collective-permute-done((bf16[16,512]{1,0:T(8,128)(2,1)S(1)}, bf16[16,512]{1,0:T(8,128)(2,1)S(1)}, u32[]{:S(2)}, u32[]{:S(2)}) %collective-permute-start.2) | collective-permute-done | bytes 16416 | tf_op jit(solution)/shard_map/ppermute | solution.py:192
  33.8 3.1 %gather_fusion.5 = f32[768,512]{1,0:T(8,128)} fusion(f32[256,512]{1,0:T(8,128)S(1)} %fusion.74, s32[1024]{0:T(1024)S(1)} %pad_clamp_fusion), kind=kCustom, calls=%fused_computation.5 | custom fusion | bytes 3148800 | tf_op jit(solution)/shard_map/gather | solution.py:50
  36.9 0.9 collective-permute-done.3
  37.9 0.6 gather_fusion.3
  38.7 3.1 %gather_fusion.4 = f32[768,512]{1,0:T(8,128)} fusion(f32[320,512]{1,0:T(8,128)S(1)} %pad_maximum_fusion, s32[1024]{0:T(1024)S(1)} %pad_clamp_fusion.1), kind=kCustom, calls=%fused_computation.4 | custom fusion | bytes 3148800 | tf_op jit(solution)/shard_map/gather | solution.py:50
  41.8 2.9 %fusion.70 = (f32[256]{0:T(256)S(1)}, f32[256,512]{1,0:T(8,128)S(1)}) fusion(bf16[512,512]{1,0:T(8,128)(2,1)} %param.36, f32[768,512]{1,0:T(8,128)} %gather_fusion.4, f32[768,512]{1,0:T(8,128)} %gather_fusion.5, s32[768]{0:T(1024)S(1)} %copy-done.10, pred[768]{0:T(1024)(128)(4,1)S(1)} %iota_compare_fusion.8), kind=kOutput, calls=%fused_computation.122 | convolution fusion | flops 607256320 | bytes 4199168 | tf_op jit(solution)/shard_map/dot_general | solution.py:57
  45.5 3.3 %gather_fusion.6 = bf16[768,512]{1,0:T(8,128)(2,1)} fusion(bf16[256,512]{1,0:T(8,128)(2,1)S(1)} %fusion.33, s32[1024]{0:T(1024)S(1)} %pad_clamp_fusion), kind=kCustom, calls=%fused_computation.6 | custom fusion | bytes 1575936 | tf_op jit(solution)/shard_map/gather | solution.py:64
  48.8 3.2 %multiply_convert_fusion.1 = bf16[768,512]{1,0:T(8,128)(2,1)S(1)} fusion(bf16[512,512]{1,0:T(8,128)(2,1)} %param.36, bf16[768,512]{1,0:T(8,128)(2,1)} %gather_fusion.6, pred[768]{0:T(1024)(128)(4,1)S(1)} %iota_compare_fusion.8, f32[768,512]{1,0:T(8,128)} %gather_fusion.4, f32[768,512]{1,0:T(8,128)} %gather_fusion.5), kind=kOutput, calls=%fused_computation.13 | convolution fusion | flops 406978560 | bytes 5243648 | tf_op jit(solution)/shard_map/dot_general | solution.py:65
  52.0 0.9 copy-done.6
  53.4 1.3 %fusion.54 = f32[64,512]{1,0:T(8,128)} fusion(bf16[512,512]{1,0:T(8,128)(2,1)S(1)} %copy-done.1, f32[320,512]{1,0:T(8,128)S(1)} %fusion.6), kind=kOutput, calls=%fused_computation.80 | convolution fusion | flops 201326592 | bytes 786432 | tf_op jit(solution)/shard_map/dot_general | solution.py:224
  55.0 1.7 %convolution_add_fusion.1 = f32[256,512]{1,0:T(8,128)S(1)} fusion(f32[256,512]{1,0:T(8,128)S(1)} %convolution_add_fusion.2, bf16[512,512]{1,0:T(8,128)(2,1)S(1)} %copy-done.4, bf16[768,512]{1,0:T(8,128)(2,1)} %copy-done.6, s32[768]{0:T(1024)S(1)} %copy-done.10, pred[768]{0:T(1024)(128)(4,1)} %copy-done.22), kind=kOutput, calls=%fused_computation.25 | convolution fusion | flops 336199680 | bytes 2363136 | tf_op jit(solution)/shard_map/dot_general | solution.py:140
  56.7 17.4 %reduce-scatter.2.cloned.1.call-done = f32[16,512]{1,0:T(8,128)} async-done(((f32[64,512]{1,0:T(8,128)}), f32[16,512]{1,0:T(8,128)}) %reduce-scatter.2.cloned.1.call-update) | async-done | bytes 32784 | tf_op jit(solution)/shard_map/reduce_scatter | solution.py:223
  74.2 0.8 fusion.56
  75.4 2.7 %gather_fusion.7 = bf16[768,512]{1,0:T(8,128)(2,1)S(1)} fusion(bf16[256,512]{1,0:T(8,128)(2,1)S(1)} %subtract_multiply_fusion, s32[1024]{0:T(1024)S(1)} %pad_clamp_fusion.3), kind=kCustom, calls=%fused_computation.7 | custom fusion | bytes 1575936 | tf_op jit(solution)/shard_map/gather | solution.py:64
  78.2 3.8 %multiply_convert_fusion = bf16[768,512]{1,0:T(8,128)(2,1)} fusion(bf16[512,512]{1,0:T(8,128)(2,1)S(1)} %copy-done.23, bf16[768,512]{1,0:T(8,128)(2,1)S(1)} %gather_fusion.7, pred[768]{0:T(1024)(128)(4,1)S(1)} %copy-done.25, f32[768,512]{1,0:T(8,128)} %gather_fusion.1, f32[768,512]{1,0:T(8,128)} %gather_fusion.2), kind=kOutput, calls=%fused_computation.11 | convolution fusion | flops 406978560 | bytes 5243648 | tf_op jit(solution)/shard_map/dot_general | solution.py:65
  81.9 2.5 %fusion.4 = bf16[256,512]{1,0:T(8,128)(2,1)} fusion(f32[256,512]{1,0:T(8,128)S(1)} %fusion.56, bf16[512,512]{1,0:T(8,128)(2,1)S(1)} %copy-done.8, bf16[768,512]{1,0:T(8,128)(2,1)} %multiply_convert_fusion, s32[768]{0:T(1024)S(1)} %copy-done.19, pred[768]{0:T(1024)(128)(4,1)S(1)} %copy-done.25), kind=kOutput, calls=%fused_computation.27 | convolution fusion | flops 336330752 | bytes 2100992 | tf_op jit(solution)/shard_map/dot_general | solution.py:104
  84.4 0.8 fusion.1
  85.3 4.2 %collective-permute-start.5 = (bf16[128,512]{1,0:T(8,128)(2,1)S(1)}, bf16[128,512]{1,0:T(8,128)(2,1)S(1)}, u32[]{:S(2)}, u32[]{:S(2)}) collective-permute-start(bf16[128,512]{1,0:T(8,128)(2,1)S(1)} %get-tuple-element.18), channel_id=1, source_target_pairs={{0,4},{4,8},{8,12},{12,16},{16,20},{20,24},{24,28},{28,0},{1,5},{5... | collective-permute-start | bytes 393224 | tf_op jit(solution)/shard_map/ppermute | solution.py:22
  89.5 0.5 fusion.35
  89.9 1.5 %collective-permute-done.5 = bf16[128,512]{1,0:T(8,128)(2,1)S(1)} collective-permute-done((bf16[128,512]{1,0:T(8,128)(2,1)S(1)}, bf16[128,512]{1,0:T(8,128)(2,1)S(1)}, u32[]{:S(2)}, u32[]{:S(2)}) %collective-permute-start.5) | collective-permute-done | bytes 131104 | tf_op jit(solution)/shard_map/ppermute | solution.py:22
  91.4 3.0 %collective-permute-done.6 = bf16[128,512]{1,0:T(8,128)(2,1)S(1)} collective-permute-done((bf16[128,512]{1,0:T(8,128)(2,1)S(1)}, bf16[128,512]{1,0:T(8,128)(2,1)S(1)}, u32[]{:S(2)}, u32[]{:S(2)}) %collective-permute-start.6) | collective-permute-done | bytes 131104 | tf_op jit(solution)/shard_map/ppermute | solution.py:23
  94.8 2.5 %scatter_fusion = f32[512,512]{1,0:T(8,128)S(1)} fusion(f32[512,512]{1,0:T(8,128)S(1)} %fusion.35, s32[256]{0:T(256)S(1)} %copy-done.14, f32[256,512]{1,0:T(8,128)S(1)} %fusion.50), kind=kCustom, calls=%fused_computation.8 | custom fusion | flops 131072 | bytes 1573888 | tf_op jit(solution)/shard_map/scatter-add | solution.py:251
  97.3 0.9 convert_element_type.67
  (100 shorter events, 4.1 us)
Async XLA Ops:
  7.2 11.5 %copy-start = (bf16[512,512]{1,0:T(8,128)(2,1)S(1)}, bf16[512,512]{1,0:T(8,128)(2,1)}, u32[]{:S(2)}) copy-start(bf16[512,512]{1,0:T(8,128)(2,1)} %param.30) | copy-start | bytes 1572868
  7.2 7.8 %copy-start.20 = (s32[768]{0:T(1024)S(1)}, s32[768]{0:T(1024)}, u32[]{:S(2)}) copy-start(s32[768]{0:T(1024)} %param.24) | copy-start | bytes 9220
  7.2 7.9 %copy-start.16 = (s32[768]{0:T(1024)S(1)}, s32[768]{0:T(1024)}, u32[]{:S(2)}) copy-start(s32[768]{0:T(1024)} %param.27) | copy-start | bytes 9220
  7.2 7.9 %copy-start.18 = (s32[768]{0:T(1024)S(1)}, s32[768]{0:T(1024)}, u32[]{:S(2)}) copy-start(s32[768]{0:T(1024)} %param.25) | copy-start | bytes 9220
  7.2 7.9 %copy-start.10 = (s32[768]{0:T(1024)S(1)}, s32[768]{0:T(1024)}, u32[]{:S(2)}) copy-start(s32[768]{0:T(1024)} %param.28) | copy-start | bytes 9220
  7.2 7.9 %copy-start.7 = (bf16[512,512]{1,0:T(8,128)(2,1)S(1)}, bf16[512,512]{1,0:T(8,128)(2,1)}, u32[]{:S(2)}) copy-start(bf16[512,512]{1,0:T(8,128)(2,1)} %param.31) | copy-start | bytes 1572868
  7.2 7.9 %copy-start.5 = (bf16[256,512]{1,0:T(8,128)(2,1)S(1)}, bf16[256,512]{1,0:T(8,128)(2,1)}, u32[]{:S(2)}) copy-start(bf16[256,512]{1,0:T(8,128)(2,1)} %param.21) | copy-start | bytes 786436
  7.2 66.9 %reduce-scatter.2.cloned.1.call-start = ((), (), s32[]{:S(2)}) async-start(), calls=%async_computation.1 | async-start | bytes 163840 | tf_op jit(solution)/shard_map/reduce_scatter | solution.py:223
  11.0 7.6 %collective-permute-start = (bf16[128,512]{1,0:T(8,128)(2,1)S(1)}, bf16[128,512]{1,0:T(8,128)(2,1)S(1)}, u32[]{:S(2)}, u32[]{:S(2)}) collective-permute-start(bf16[128,512]{1,0:T(8,128)(2,1)S(1)} %get-tuple-element.22), channel_id=1, source_target_pairs={{0,4},{4,8},{8,12},{12,16},{16,20},{20,24},{24,28},{28,0},{1,5},{5... | collective-permute-start | bytes 393224 | tf_op jit(solution)/shard_map/ppermute | solution.py:22
  13.7 5.0 %collective-permute-start.1 = (bf16[128,512]{1,0:T(8,128)(2,1)S(1)}, bf16[128,512]{1,0:T(8,128)(2,1)S(1)}, u32[]{:S(2)}, u32[]{:S(2)}) collective-permute-start(bf16[128,512]{1,0:T(8,128)(2,1)S(1)} %get-tuple-element.23), channel_id=1, source_target_pairs={{4,0},{8,4},{12,8},{16,12},{20,16},{24,20},{28,24},{0,28},{5,1},{9... | collective-permute-start | bytes 393224 | tf_op jit(solution)/shard_map/ppermute | solution.py:23
  15.0 7.4 %copy-start.24 = (pred[768]{0:T(1024)(128)(4,1)}, pred[768]{0:T(1024)(128)(4,1)S(1)}, u32[]{:S(2)}) copy-start(pred[768]{0:T(1024)(128)(4,1)S(1)} %iota_compare_fusion.9) | copy-start | bytes 2308
  15.5 33.3 %copy-start.22 = (pred[768]{0:T(1024)(128)(4,1)}, pred[768]{0:T(1024)(128)(4,1)S(1)}, u32[]{:S(2)}) copy-start(pred[768]{0:T(1024)(128)(4,1)S(1)} %iota_compare_fusion.8) | copy-start | bytes 2308
  15.5 3.2 %copy-start.2 = (bf16[512,512]{1,0:T(8,128)(2,1)S(1)}, bf16[512,512]{1,0:T(8,128)(2,1)}, u32[]{:S(2)}) copy-start(bf16[512,512]{1,0:T(8,128)(2,1)} %param.20) | copy-start | bytes 1572868
  22.4 3.1 %copy-start.9 = (f32[512]{0:T(512)S(1)}, f32[512]{0:T(512)}, u32[]{:S(2)}) copy-start(f32[512]{0:T(512)} %param.33) | copy-start | bytes 6148
  25.3 3.8 %copy-start.4 = (bf16[512,512]{1,0:T(8,128)(2,1)S(1)}, bf16[512,512]{1,0:T(8,128)(2,1)}, u32[]{:S(2)}) copy-start(bf16[512,512]{1,0:T(8,128)(2,1)} %param.35) | copy-start | bytes 1572868
  25.3 8.2 %copy-start.1 = (bf16[512,512]{1,0:T(8,128)(2,1)S(1)}, bf16[512,512]{1,0:T(8,128)(2,1)}, u32[]{:S(2)}) copy-start(bf16[512,512]{1,0:T(8,128)(2,1)} %param.34) | copy-start | bytes 1572868
  25.5 8.3 %copy-start.11 = (f32[256]{0:T(256)}, f32[256]{0:T(256)S(1)}, u32[]{:S(2)}) copy-start(f32[256]{0:T(256)S(1)} %add_rsqrt_fusion.1) | copy-start | bytes 3076
  25.7 11.2 %collective-permute-start.4 = (bf16[16,512]{1,0:T(8,128)(2,1)S(1)}, bf16[16,512]{1,0:T(8,128)(2,1)S(1)}, u32[]{:S(2)}, u32[]{:S(2)}) collective-permute-start(bf16[16,512]{1,0:T(8,128)(2,1)S(1)} %get-tuple-element.21), channel_id=1, source_target_pairs={{1,0},{2,1},{3,2},{0,3},{5,4},{6,5},{7,6},{4,7},{9,8},{10,9},{11,1... | collective-permute-start | bytes 49160 | tf_op jit(solution)/shard_map/ppermute | solution.py:195
  29.1 4.4 %collective-permute-start.2 = (bf16[16,512]{1,0:T(8,128)(2,1)S(1)}, bf16[16,512]{1,0:T(8,128)(2,1)S(1)}, u32[]{:S(2)}, u32[]{:S(2)}) collective-permute-start(bf16[16,512]{1,0:T(8,128)(2,1)S(1)} %get-tuple-element.21), channel_id=1, source_target_pairs={{0,1},{1,2},{2,3},{3,0},{4,5},{5,6},{6,7},{7,4},{8,9},{9,10},{10,1... | collective-permute-start | bytes 49160 | tf_op jit(solution)/shard_map/ppermute | solution.py:192
  33.5 4.4 %collective-permute-start.3 = (bf16[16,512]{1,0:T(8,128)(2,1)S(1)}, bf16[16,512]{1,0:T(8,128)(2,1)S(1)}, u32[]{:S(2)}, u32[]{:S(2)}) collective-permute-start(bf16[16,512]{1,0:T(8,128)(2,1)S(1)} %collective-permute-done.2), channel_id=1, source_target_pairs={{0,1},{1,2},{2,3},{3,0},{4,5},{5,6},{6,7},{7,4},{8,9},{9,10},{10,1... | collective-permute-start | bytes 49160 | tf_op jit(solution)/shard_map/ppermute | solution.py:192
  41.8 3.2 %copy-start.3 = (bf16[256,512]{1,0:T(8,128)(2,1)S(1)}, bf16[256,512]{1,0:T(8,128)(2,1)}, u32[]{:S(2)}) copy-start(bf16[256,512]{1,0:T(8,128)(2,1)} %param.22) | copy-start | bytes 786436
  41.8 3.2 %copy-start.15 = (f32[512]{0:T(512)S(1)}, f32[512]{0:T(512)}, u32[]{:S(2)}) copy-start(f32[512]{0:T(512)} %param.37) | copy-start | bytes 6148
  48.8 4.1 %copy-start.17 = (s32[768]{0:T(1024)S(1)}, s32[768]{0:T(1024)}, u32[]{:S(2)}) copy-start(s32[768]{0:T(1024)} %param.27) | copy-start | bytes 9220
  55.0 20.0 %copy-start.12 = (f32[256]{0:T(256)S(1)}, f32[256]{0:T(256)}, u32[]{:S(2)}) copy-start(f32[256]{0:T(256)} %copy-done.11) | copy-start | bytes 3076
  75.4 2.7 %copy-start.23 = (bf16[512,512]{1,0:T(8,128)(2,1)S(1)}, bf16[512,512]{1,0:T(8,128)(2,1)}, u32[]{:S(2)}) copy-start(bf16[512,512]{1,0:T(8,128)(2,1)} %param.32) | copy-start | bytes 1572868
  75.4 2.7 %copy-start.25 = (pred[768]{0:T(1024)(128)(4,1)S(1)}, pred[768]{0:T(1024)(128)(4,1)}, u32[]{:S(2)}) copy-start(pred[768]{0:T(1024)(128)(4,1)} %copy-done.24) | copy-start | bytes 2308
  78.1 3.8 %copy-start.8 = (bf16[512,512]{1,0:T(8,128)(2,1)S(1)}, bf16[512,512]{1,0:T(8,128)(2,1)}, u32[]{:S(2)}) copy-start(bf16[512,512]{1,0:T(8,128)(2,1)} %param.31) | copy-start | bytes 1572868
  78.1 3.8 %copy-start.19 = (s32[768]{0:T(1024)S(1)}, s32[768]{0:T(1024)}, u32[]{:S(2)}) copy-start(s32[768]{0:T(1024)} %param.25) | copy-start | bytes 9220
  81.9 2.5 %copy-start.21 = (s32[768]{0:T(1024)S(1)}, s32[768]{0:T(1024)}, u32[]{:S(2)}) copy-start(s32[768]{0:T(1024)} %param.24) | copy-start | bytes 9220
  85.3 6.1 %collective-permute-start.5 = (bf16[128,512]{1,0:T(8,128)(2,1)S(1)}, bf16[128,512]{1,0:T(8,128)(2,1)S(1)}, u32[]{:S(2)}, u32[]{:S(2)}) collective-permute-start(bf16[128,512]{1,0:T(8,128)(2,1)S(1)} %get-tuple-element.18), channel_id=1, source_target_pairs={{0,4},{4,8},{8,12},{12,16},{16,20},{20,24},{24,28},{28,0},{1,5},{5... | collective-permute-start | bytes 393224 | tf_op jit(solution)/shard_map/ppermute | solution.py:22
  89.5 5.3 %copy-start.14 = (s32[256]{0:T(256)S(1)}, s32[256]{0:T(256)}, u32[]{:S(2)}) copy-start(s32[256]{0:T(256)} %copy-done.13) | copy-start | bytes 3076
  89.5 5.0 %collective-permute-start.6 = (bf16[128,512]{1,0:T(8,128)(2,1)S(1)}, bf16[128,512]{1,0:T(8,128)(2,1)S(1)}, u32[]{:S(2)}, u32[]{:S(2)}) collective-permute-start(bf16[128,512]{1,0:T(8,128)(2,1)S(1)} %get-tuple-element.19), channel_id=1, source_target_pairs={{4,0},{8,4},{12,8},{16,12},{20,16},{24,20},{28,24},{0,28},{5,1},{9... | collective-permute-start | bytes 393224 | tf_op jit(solution)/shard_map/ppermute | solution.py:23
  (3 other events, 4.0 us)
Sparse Core Ops, SparseCore 0:
  55.1 18.9 reduce-scatter.1
